TPU v7x, 32 devices: a whole 2x2x4 slice. The times are simulated.
32 devices in a mesh: row: 8 (over y, x, core), col: 4 (over z).
Axes of the slice: x: 2, y: 2, z: 4, core: 2. Of those that a mesh axis runs over, the one named last changes fastest.
Arguments:
- upper_block: float32 [2, 1024, 1024], P(None, 'row', 'col'), may hold values from -0.1875 to 0.1875
- block_inverse: float32 [2, 1024, 128], P(None, 'row'), may hold values from -0.25 to 0.25
- panel_rhs: float32 [2, 32, 1024], P(None, None, 'row'), may hold values from -6 to 6
- upper_trail: float32 [2, 1024, 65536], P(None, 'row', 'col'), may hold values from -0.125 to 0.125
- trail_rhs: float32 [2, 32, 65536], P(None, None, ('col', 'row')), may hold values from -6 to 6
- currents: float32 [2, 1024], P(None, 'row'), may hold values from -4 to 4
- owner: int32 [1024], P('row'), may hold values from 0 to 127
Outputs:
- panel_adjoint: float32 [2, 32, 1024], P(None, None, 'row')
- trail_updated: float32 [2, 32, 65536], P(None, None, ('col', 'row'))
- patch_gradient: float32 [128], P(('row', 'col'))
Inputs may be any that keep to these rules, and one draw needn't show every extreme that they name: owner names a surface patch for each panel unknown.
All inputs are finite; a program needn't handle non-finite values.
Results may differ from a plain program's by a relative error of at most 0.0003.
Values sent between devices are 32-bit elements; how exact they have to be, the bound alone decides.
No kernel may reach another device: no remote copies, remote signals or barrier semaphores. Data moves between devices by JAX's collectives and lax.ppermute only.
A program may use at most 64 MiB of HBM per device.

v0:
```python
import jax
import jax.numpy as jnp
from jax import lax
from jax.sharding import PartitionSpec as P

PATCH_DEV = 4
highest = lax.Precision.HIGHEST


def shifted(block, axis, distance):
    devices = range(lax.axis_size(axis))
    route = [(i - distance, i) for i in devices if i - distance in devices]
    return lax.ppermute(block, axis, route)


def from_root(value, axis, source):
    kept = jnp.where(lax.axis_index(axis) == source, value, 0).astype(value.dtype)
    return lax.psum(kept, axis)


def product_high(first, second):
    return jnp.dot(first, second, precision=highest, preferred_element_type=jnp.float32)


def conj_product(left, right):
    real_part = product_high(left[0], right[0]) + product_high(left[1], right[1])
    imag_part = product_high(left[1], right[0]) - product_high(left[0], right[1])
    return jnp.stack([real_part, imag_part])


def on_device(upper_block, block_inverse, panel_rhs, upper_trail, trail_rhs, currents, owner):
    rows_count = lax.axis_size("row")
    cols_count = lax.axis_size("col")
    row_index = lax.axis_index("row")
    col_index = lax.axis_index("col")
    width = block_inverse.shape[1]
    quarter = upper_block.shape[2]
    observers = panel_rhs.shape[1]
    offset = row_index * width % quarter
    root_col = row_index * width // quarter

    def advance(index, carry):
        held, solved = carry
        incoming = shifted(held, "row", 1)
        local = lax.dynamic_slice_in_dim(incoming, offset, width, 2)
        candidate = conj_product(panel_rhs - local, block_inverse)
        shared = from_root(candidate, "col", root_col)
        update = conj_product(shared, upper_block)
        active = row_index == index
        held = jnp.where(active, incoming + update, held)
        solved = jnp.where(active, shared, solved)
        return (held, solved)

    held_start = jnp.zeros((2, observers, quarter), jnp.float32)
    solved_start = jnp.zeros((2, observers, width), jnp.float32)
    solved = lax.fori_loop(0, rows_count, advance, (held_start, solved_start))[1]
    term = conj_product(solved, upper_trail)
    reduced = lax.psum_scatter(term, "row", scatter_dimension=2, tiled=True)
    updated = trail_rhs - reduced
    share = width // cols_count
    start = col_index * share
    mine = lax.dynamic_slice_in_dim(solved, start, share, 2)
    total = jnp.sum(mine, axis=1)
    current_part = lax.dynamic_slice_in_dim(currents, start, share, 1)
    owner_part = lax.dynamic_slice_in_dim(owner, start, share, 0)
    partial_value = current_part[0] * total[0] - current_part[1] * total[1]
    patch_count = PATCH_DEV * rows_count * cols_count
    patch_ids = lax.broadcasted_iota(jnp.int32, (share, patch_count), 1)
    selector = (owner_part[:, None] == patch_ids).astype(jnp.float32)
    spread = product_high(partial_value[None, :], selector)[0]
    gradient = lax.psum_scatter(spread, ("row", "col"), scatter_dimension=0, tiled=True)
    return (solved, updated, gradient)


def solution(mesh):
    in_specs = (
        P(None, "row", "col"),
        P(None, "row", None),
        P(None, None, "row"),
        P(None, "row", "col"),
        P(None, None, ("col", "row")),
        P(None, "row"),
        P("row"),
    )
    out_specs = (P(None, None, "row"), P(None, None, ("col", "row")), P(("row", "col")))
    return jax.shard_map(
        on_device, mesh=mesh, in_specs=in_specs, out_specs=out_specs, check_vma=False
    )
```

profile of v0, /device:TPU:0, one launch (start us, length us, event | category | flops | bytes accessed | tf_op | source)
XLA Modules:
  0.0 354.7 jit_solution(6087188050505130230)
XLA Ops:
  7.3 249.4 %while.18 = (s32[]{:T(128)}, f32[2,32,256]{2,1,0:T(8,128)S(1)}, f32[2,32,128]{2,1,0:T(8,128)S(1)}, s32[]{:T(128)}, s32[]{:T(128)}, /*index=5*/s32[]{:T(128)}, f3...) while((s32[]{:T(128)}, f32[2,32,256]{2,1,0:T(8,128)S(1)}, ...), condition=%wide.region_2.3_spmd.clone, body=%wide.region_0.2_spmd.clone.sunk | while | flops 75653120 | bytes 2195678 | solution.py:56
  7.3 2.4 collective-permute-start
  15.5 20.1 %psum.16 = f32[2,32,128]{2,1,0:T(8,128)S(1)} all-reduce(f32[2,32,128]{2,1,0:T(8,128)S(1)} %maximum_select_fusion.2), channel_id=1, replica_groups=mesh['row'=8,'col'=4] {'col'}, use_global_device_ids=true, to_apply=%region_1.1 | all-reduce | flops 8192 | bytes 65536 | tf_op jit(solution)/shard_map/while/body/eval_jaxpr/psum | solution.py:18
  35.6 1.1 fusion.83
  37.8 1.1 fusion.84
  38.9 1.1 fusion.82
  40.0 1.3 collective-permute-start
  47.1 15.8 %psum.16 = f32[2,32,128]{2,1,0:T(8,128)S(1)} all-reduce(f32[2,32,128]{2,1,0:T(8,128)S(1)} %maximum_select_fusion.2), channel_id=1, replica_groups=mesh['row'=8,'col'=4] {'col'}, use_global_device_ids=true, to_apply=%region_1.1 | all-reduce | flops 8192 | bytes 65536 | tf_op jit(solution)/shard_map/while/body/eval_jaxpr/psum | solution.py:18
  63.0 1.1 fusion.83
  65.2 1.1 fusion.84
  66.2 1.1 fusion.82
  67.4 4.1 %collective-permute-start = (f32[2,32,256]{2,1,0:T(8,128)S(1)}, f32[2,32,256]{2,1,0:T(8,128)S(1)}, u32[]{:S(2)}, u32[]{:S(2)}) collective-permute-start(f32[2,32,256]{2,1,0:T(8,128)S(1)} %broadcast_select_fusion.2), channel_id=1, source_target_pairs={{0,4},{4,8},{8,12},{12,16},{16,20},{20,24},{24,28},{1,5},{5,9},{9,... | collective-permute-start | bytes 196616 | tf_op jit(solution)/shard_map/while/body/eval_jaxpr/ppermute | solution.py:13
  77.3 17.4 %psum.16 = f32[2,32,128]{2,1,0:T(8,128)S(1)} all-reduce(f32[2,32,128]{2,1,0:T(8,128)S(1)} %maximum_select_fusion.2), channel_id=1, replica_groups=mesh['row'=8,'col'=4] {'col'}, use_global_device_ids=true, to_apply=%region_1.1 | all-reduce | flops 8192 | bytes 65536 | tf_op jit(solution)/shard_map/while/body/eval_jaxpr/psum | solution.py:18
  94.7 1.1 fusion.83
  96.9 1.1 fusion.84
  98.0 1.1 fusion.82
  99.2 4.4 %collective-permute-start = (f32[2,32,256]{2,1,0:T(8,128)S(1)}, f32[2,32,256]{2,1,0:T(8,128)S(1)}, u32[]{:S(2)}, u32[]{:S(2)}) collective-permute-start(f32[2,32,256]{2,1,0:T(8,128)S(1)} %broadcast_select_fusion.2), channel_id=1, source_target_pairs={{0,4},{4,8},{8,12},{12,16},{16,20},{20,24},{24,28},{1,5},{5,9},{9,... | collective-permute-start | bytes 196616 | tf_op jit(solution)/shard_map/while/body/eval_jaxpr/ppermute | solution.py:13
  109.4 16.2 %psum.16 = f32[2,32,128]{2,1,0:T(8,128)S(1)} all-reduce(f32[2,32,128]{2,1,0:T(8,128)S(1)} %maximum_select_fusion.2), channel_id=1, replica_groups=mesh['row'=8,'col'=4] {'col'}, use_global_device_ids=true, to_apply=%region_1.1 | all-reduce | flops 8192 | bytes 65536 | tf_op jit(solution)/shard_map/while/body/eval_jaxpr/psum | solution.py:18
  125.5 1.1 fusion.83
  127.7 1.1 fusion.84
  128.8 1.1 fusion.82
  130.0 4.6 %collective-permute-start = (f32[2,32,256]{2,1,0:T(8,128)S(1)}, f32[2,32,256]{2,1,0:T(8,128)S(1)}, u32[]{:S(2)}, u32[]{:S(2)}) collective-permute-start(f32[2,32,256]{2,1,0:T(8,128)S(1)} %broadcast_select_fusion.2), channel_id=1, source_target_pairs={{0,4},{4,8},{8,12},{12,16},{16,20},{20,24},{24,28},{1,5},{5,9},{9,... | collective-permute-start | bytes 196616 | tf_op jit(solution)/shard_map/while/body/eval_jaxpr/ppermute | solution.py:13
  140.4 17.7 %psum.16 = f32[2,32,128]{2,1,0:T(8,128)S(1)} all-reduce(f32[2,32,128]{2,1,0:T(8,128)S(1)} %maximum_select_fusion.2), channel_id=1, replica_groups=mesh['row'=8,'col'=4] {'col'}, use_global_device_ids=true, to_apply=%region_1.1 | all-reduce | flops 8192 | bytes 65536 | tf_op jit(solution)/shard_map/while/body/eval_jaxpr/psum | solution.py:18
  158.0 1.1 fusion.83
  160.2 1.1 fusion.84
  161.3 1.1 fusion.82
  162.5 4.3 %collective-permute-start = (f32[2,32,256]{2,1,0:T(8,128)S(1)}, f32[2,32,256]{2,1,0:T(8,128)S(1)}, u32[]{:S(2)}, u32[]{:S(2)}) collective-permute-start(f32[2,32,256]{2,1,0:T(8,128)S(1)} %broadcast_select_fusion.2), channel_id=1, source_target_pairs={{0,4},{4,8},{8,12},{12,16},{16,20},{20,24},{24,28},{1,5},{5,9},{9,... | collective-permute-start | bytes 196616 | tf_op jit(solution)/shard_map/while/body/eval_jaxpr/ppermute | solution.py:13
  172.5 16.6 %psum.16 = f32[2,32,128]{2,1,0:T(8,128)S(1)} all-reduce(f32[2,32,128]{2,1,0:T(8,128)S(1)} %maximum_select_fusion.2), channel_id=1, replica_groups=mesh['row'=8,'col'=4] {'col'}, use_global_device_ids=true, to_apply=%region_1.1 | all-reduce | flops 8192 | bytes 65536 | tf_op jit(solution)/shard_map/while/body/eval_jaxpr/psum | solution.py:18
  189.1 1.1 fusion.83
  191.3 1.1 fusion.84
  192.4 1.1 fusion.82
  193.6 4.2 %collective-permute-start = (f32[2,32,256]{2,1,0:T(8,128)S(1)}, f32[2,32,256]{2,1,0:T(8,128)S(1)}, u32[]{:S(2)}, u32[]{:S(2)}) collective-permute-start(f32[2,32,256]{2,1,0:T(8,128)S(1)} %broadcast_select_fusion.2), channel_id=1, source_target_pairs={{0,4},{4,8},{8,12},{12,16},{16,20},{20,24},{24,28},{1,5},{5,9},{9,... | collective-permute-start | bytes 196616 | tf_op jit(solution)/shard_map/while/body/eval_jaxpr/ppermute | solution.py:13
  203.5 17.5 %psum.16 = f32[2,32,128]{2,1,0:T(8,128)S(1)} all-reduce(f32[2,32,128]{2,1,0:T(8,128)S(1)} %maximum_select_fusion.2), channel_id=1, replica_groups=mesh['row'=8,'col'=4] {'col'}, use_global_device_ids=true, to_apply=%region_1.1 | all-reduce | flops 8192 | bytes 65536 | tf_op jit(solution)/shard_map/while/body/eval_jaxpr/psum | solution.py:18
  221.1 1.1 fusion.83
  223.3 1.1 fusion.84
  224.3 1.1 fusion.82
  225.5 4.4 %collective-permute-start = (f32[2,32,256]{2,1,0:T(8,128)S(1)}, f32[2,32,256]{2,1,0:T(8,128)S(1)}, u32[]{:S(2)}, u32[]{:S(2)}) collective-permute-start(f32[2,32,256]{2,1,0:T(8,128)S(1)} %broadcast_select_fusion.2), channel_id=1, source_target_pairs={{0,4},{4,8},{8,12},{12,16},{16,20},{20,24},{24,28},{1,5},{5,9},{9,... | collective-permute-start | bytes 196616 | tf_op jit(solution)/shard_map/while/body/eval_jaxpr/ppermute | solution.py:13
  235.7 16.6 %psum.16 = f32[2,32,128]{2,1,0:T(8,128)S(1)} all-reduce(f32[2,32,128]{2,1,0:T(8,128)S(1)} %maximum_select_fusion.2), channel_id=1, replica_groups=mesh['row'=8,'col'=4] {'col'}, use_global_device_ids=true, to_apply=%region_1.1 | all-reduce | flops 8192 | bytes 65536 | tf_op jit(solution)/shard_map/while/body/eval_jaxpr/psum | solution.py:18
  254.5 1.1 fusion.84
  255.6 1.1 fusion.82
  256.8 6.9 %fusion.29 = f32[32,16384]{1,0:T(8,128)S(1)} fusion(f32[2,128,16384]{2,1,0:T(8,128)} %param.12, f32[2,32,128]{2,1,0:T(8,128)S(1)} %get-tuple-element.224), kind=kOutput, calls=%fused_computation.44 | convolution fusion | flops 805306368 | bytes 10502144 | tf_op jit(solution)/shard_map/dot_general | solution.py:22
  263.6 7.2 %fusion.31 = f32[32,16384]{1,0:T(8,128)S(1)} fusion(f32[2,128,16384]{2,1,0:T(8,128)} %param.12, f32[2,32,128]{2,1,0:T(8,128)S(1)} %get-tuple-element.224), kind=kOutput, calls=%fused_computation.46 | convolution fusion | flops 805306368 | bytes 10502144 | tf_op jit(solution)/shard_map/dot_general | solution.py:22
  270.9 4.4 %fusion.25 = f32[1,32,16384]{2,1,0:T(8,128)S(1)} fusion(f32[32,16384]{1,0:T(8,128)S(1)} %fusion.29, f32[2,128,16384]{2,1,0:T(8,128)S(1)} %copy-done.1, f32[2,32,128]{2,1,0:T(8,128)S(1)} %get-tuple-element.224), kind=kOutput, calls=%fused_computation.39 | convolution fusion | flops 805830656 | bytes 12599296 | tf_op jit(solution)/shard_map/dot_general | solution.py:22
  275.3 4.4 %fusion.26 = f32[1,32,16384]{2,1,0:T(8,128)S(1)} fusion(f32[32,16384]{1,0:T(8,128)S(1)} %fusion.31, f32[2,128,16384]{2,1,0:T(8,128)S(1)} %copy-done.1, f32[2,32,128]{2,1,0:T(8,128)S(1)} %get-tuple-element.224), kind=kOutput, calls=%fused_computation.41 | convolution fusion | flops 805830656 | bytes 12599296 | tf_op jit(solution)/shard_map/dot_general | solution.py:22
  279.8 2.2 pad_maximum_fusion
  283.1 51.4 %all-reduce = f32[128]{0:T(128)S(1)} all-reduce(f32[128]{0:T(128)S(1)} %convolution_bitcast_fusion), channel_id=3, replica_groups=mesh['row'=8,'col'=4] {'row','col'}, use_global_device_ids=true, to_apply=%region_5.6.clone | all-reduce | flops 128 | bytes 1024
  335.0 10.9 %reduce-scatter.2.cloned.1.call-done = f32[2,32,2048]{2,1,0:T(8,128)} async-done(((f32[2,32,16384]{2,1,0:T(8,128)}), f32[2,32,2048]{2,1,0:T(8,128)}) %reduce-scatter.2.cloned.1.call-update) | async-done | bytes 524304 | tf_op jit(solution)/shard_map/reduce_scatter | solution.py:58
  345.9 1.9 sub.46
  (108 shorter events, 57.6 us)
Async XLA Ops:
  7.2 275.6 %copy-start = (f32[2,128]{1,0:T(2,128)S(1)}, f32[2,128]{1,0:T(2,128)}, u32[]{:S(2)}) copy-start(f32[2,128]{1,0:T(2,128)} %param.14) | copy-start | bytes 3076
  7.2 338.7 %reduce-scatter.2.cloned.1.call-start = ((), (), s32[]{:S(2)}) async-start(), calls=%async_computation.1 | async-start | bytes 4718592 | tf_op jit(solution)/shard_map/reduce_scatter | solution.py:58
  7.3 3.3 collective-permute-start
  40.0 2.2 collective-permute-start
  67.4 4.9 %collective-permute-start = (f32[2,32,256]{2,1,0:T(8,128)S(1)}, f32[2,32,256]{2,1,0:T(8,128)S(1)}, u32[]{:S(2)}, u32[]{:S(2)}) collective-permute-start(f32[2,32,256]{2,1,0:T(8,128)S(1)} %broadcast_select_fusion.2), channel_id=1, source_target_pairs={{0,4},{4,8},{8,12},{12,16},{16,20},{20,24},{24,28},{1,5},{5,9},{9,... | collective-permute-start | bytes 196616 | tf_op jit(solution)/shard_map/while/body/eval_jaxpr/ppermute | solution.py:13
  99.2 5.3 %collective-permute-start = (f32[2,32,256]{2,1,0:T(8,128)S(1)}, f32[2,32,256]{2,1,0:T(8,128)S(1)}, u32[]{:S(2)}, u32[]{:S(2)}) collective-permute-start(f32[2,32,256]{2,1,0:T(8,128)S(1)} %broadcast_select_fusion.2), channel_id=1, source_target_pairs={{0,4},{4,8},{8,12},{12,16},{16,20},{20,24},{24,28},{1,5},{5,9},{9,... | collective-permute-start | bytes 196616 | tf_op jit(solution)/shard_map/while/body/eval_jaxpr/ppermute | solution.py:13
  130.0 5.5 %collective-permute-start = (f32[2,32,256]{2,1,0:T(8,128)S(1)}, f32[2,32,256]{2,1,0:T(8,128)S(1)}, u32[]{:S(2)}, u32[]{:S(2)}) collective-permute-start(f32[2,32,256]{2,1,0:T(8,128)S(1)} %broadcast_select_fusion.2), channel_id=1, source_target_pairs={{0,4},{4,8},{8,12},{12,16},{16,20},{20,24},{24,28},{1,5},{5,9},{9,... | collective-permute-start | bytes 196616 | tf_op jit(solution)/shard_map/while/body/eval_jaxpr/ppermute | solution.py:13
  162.5 5.2 %collective-permute-start = (f32[2,32,256]{2,1,0:T(8,128)S(1)}, f32[2,32,256]{2,1,0:T(8,128)S(1)}, u32[]{:S(2)}, u32[]{:S(2)}) collective-permute-start(f32[2,32,256]{2,1,0:T(8,128)S(1)} %broadcast_select_fusion.2), channel_id=1, source_target_pairs={{0,4},{4,8},{8,12},{12,16},{16,20},{20,24},{24,28},{1,5},{5,9},{9,... | collective-permute-start | bytes 196616 | tf_op jit(solution)/shard_map/while/body/eval_jaxpr/ppermute | solution.py:13
  193.6 5.1 %collective-permute-start = (f32[2,32,256]{2,1,0:T(8,128)S(1)}, f32[2,32,256]{2,1,0:T(8,128)S(1)}, u32[]{:S(2)}, u32[]{:S(2)}) collective-permute-start(f32[2,32,256]{2,1,0:T(8,128)S(1)} %broadcast_select_fusion.2), channel_id=1, source_target_pairs={{0,4},{4,8},{8,12},{12,16},{16,20},{20,24},{24,28},{1,5},{5,9},{9,... | collective-permute-start | bytes 196616 | tf_op jit(solution)/shard_map/while/body/eval_jaxpr/ppermute | solution.py:13
  225.5 5.3 %collective-permute-start = (f32[2,32,256]{2,1,0:T(8,128)S(1)}, f32[2,32,256]{2,1,0:T(8,128)S(1)}, u32[]{:S(2)}, u32[]{:S(2)}) collective-permute-start(f32[2,32,256]{2,1,0:T(8,128)S(1)} %broadcast_select_fusion.2), channel_id=1, source_target_pairs={{0,4},{4,8},{8,12},{12,16},{16,20},{20,24},{24,28},{1,5},{5,9},{9,... | collective-permute-start | bytes 196616 | tf_op jit(solution)/shard_map/while/body/eval_jaxpr/ppermute | solution.py:13
  256.7 26.0 %copy-start.2 = (f32[2,32,128]{2,1,0:T(8,128)}, f32[2,32,128]{2,1,0:T(8,128)S(1)}, u32[]{:S(2)}) copy-start(f32[2,32,128]{2,1,0:T(8,128)S(1)} %get-tuple-element.224) | copy-start | bytes 98308
  256.7 14.2 %copy-start.1 = (f32[2,128,16384]{2,1,0:T(8,128)S(1)}, f32[2,128,16384]{2,1,0:T(8,128)}, u32[]{:S(2)}) copy-start(f32[2,128,16384]{2,1,0:T(8,128)} %param.12) | copy-start | bytes 50331652
  282.0 0.7 copy-start.4
  282.0 64.0 %copy-start.3 = (f32[2,32,2048]{2,1,0:T(8,128)S(1)}, f32[2,32,2048]{2,1,0:T(8,128)}, u32[]{:S(2)}) copy-start(f32[2,32,2048]{2,1,0:T(8,128)} %param.13) | copy-start | bytes 1572868
Sparse Core Ops, SparseCore 0:
  282.1 63.7 reduce-scatter.1
where the time goes:
time: 358 us; the launch traced here: 355 us
  blocking collectives  189 us (53%)
  matrix products  89.9 us (25%)
  starting transfers between devices  29.6 us (8%)
  waiting for transfers between devices  17.8 us (5%)
  between operations  14.2 us (4%)
  other arithmetic  11.3 us (3%)
    psum x8, blocking collectives, from_root(): return lax.psum(kept, axis)  138 us
    dot_general x69, matrix products, product_high(): jnp.dot(first, second, precision=highest, preferred_element_type=jnp.floa...  89.9 us
    unnamed x1, blocking collectives  51.4 us
    ppermute x8, starting transfers between devices, shifted(): return lax.ppermute(block, axis, route)  29.6 us
    reduce_scatter x1, waiting for transfers between devices, on_device(): reduced = lax.psum_scatter(term, 'row', scatter_dimension=2, tiled=True)  10.9 us
  transfers between devices with their start and end apart: 9, of which 9 were waited for; matrix products, arithmetic and copies ran while one was open for 0% of the time, Pallas kernels for 0%

commit v1 on v0

--- a/solution.py
+++ b/solution.py
@@ -15,7 +15,7 @@
 
 def from_root(value, axis, source):
     kept = jnp.where(lax.axis_index(axis) == source, value, 0).astype(value.dtype)
-    return lax.psum(kept, axis)
+    return jnp.sum(lax.all_gather(kept, axis), axis=0)
 
 
 def product_high(first, second):

time: 358 us -> 332 us (0.927)
  blocking collectives: 189 us -> 160 us
    psum x8 -> x0, blocking collectives: 138 us -> none  [from_root(): return lax.psum(kept, axis)]
    all_gather x0 -> x8, blocking collectives: none -> 108 us  [from_root(): return jnp.sum(lax.all_gather(kept, axis), axis=0)]
where the time goes in v1:
time: 332 us; the launch traced here: 329 us
  blocking collectives  160 us (48%)
  matrix products  89.9 us (27%)
  starting transfers between devices  33.1 us (10%)
  waiting for transfers between devices  17.9 us (5%)
  between operations  14.2 us (4%)
  other arithmetic  11.4 us (3%)
    all_gather x8, blocking collectives, from_root(): return jnp.sum(lax.all_gather(kept, axis), axis=0)  108 us
    dot_general x69, matrix products, product_high(): jnp.dot(first, second, precision=highest, preferred_element_type=jnp.floa...  89.9 us
    unnamed x1, blocking collectives  51.2 us
    ppermute x8, starting transfers between devices, shifted(): return lax.ppermute(block, axis, route)  33 us
    reduce_scatter x1, waiting for transfers between devices, on_device(): reduced = lax.psum_scatter(term, 'row', scatter_dimension=2, tiled=True)  10.9 us
    ppermute x8, waiting for transfers between devices, shifted(): return lax.ppermute(block, axis, route)  6.93 us
    sub x8, other arithmetic, advance(): candidate = conj_product(panel_rhs - local, block_inverse)  6.67 us
  transfers between devices with their start and end apart: 9, of which 9 were waited for; matrix products, arithmetic and copies ran while one was open for 0% of the time, Pallas kernels for 0%

profile of v1, /device:TPU:0, one launch (start us, length us, event | category | flops | bytes accessed | tf_op | source)
XLA Modules:
  0.0 328.7 jit_solution(16046203108181132134)
XLA Ops:
  7.3 223.5 %while.18 = (s32[]{:T(128)}, f32[2,32,256]{2,1,0:T(8,128)S(1)}, f32[2,32,128]{2,1,0:T(8,128)S(1)}, s32[]{:T(128)}, s32[]{:T(128)}, /*index=5*/s32[]{:T(128)}, f3...) while((s32[]{:T(128)}, f32[2,32,256]{2,1,0:T(8,128)S(1)}, ...), condition=%wide.region_2.3_spmd.clone, body=%wide.region_0.2_spmd.clone.sunk | while | flops 75669504 | bytes 2457834 | solution.py:56
  7.3 2.4 collective-permute-start
  15.5 14.4 %all_gather.15 = f32[4,2,32,128]{3,2,1,0:T(8,128)S(1)} all-gather(f32[1,2,32,128]{3,2,1,0:T(8,128)S(1)} %maximum_select_fusion.2), channel_id=1, replica_groups=mesh['row'=8,'col'=4] {'col'}, dimensions={0}, use_global_device_ids=true | all-gather | bytes 163840 | tf_op jit(solution)/shard_map/while/body/eval_jaxpr/all_gather | solution.py:18
  31.1 1.1 fusion.81
  32.1 1.1 fusion.84
  33.2 1.1 fusion.82
  34.4 1.4 collective-permute-start
  41.6 13.4 %all_gather.15 = f32[4,2,32,128]{3,2,1,0:T(8,128)S(1)} all-gather(f32[1,2,32,128]{3,2,1,0:T(8,128)S(1)} %maximum_select_fusion.2), channel_id=1, replica_groups=mesh['row'=8,'col'=4] {'col'}, dimensions={0}, use_global_device_ids=true | all-gather | bytes 163840 | tf_op jit(solution)/shard_map/while/body/eval_jaxpr/all_gather | solution.py:18
  55.0 1.1 fusion.83
  56.1 1.1 fusion.81
  57.2 1.1 fusion.84
  58.3 1.1 fusion.82
  59.5 4.5 %collective-permute-start = (f32[2,32,256]{2,1,0:T(8,128)S(1)}, f32[2,32,256]{2,1,0:T(8,128)S(1)}, u32[]{:S(2)}, u32[]{:S(2)}) collective-permute-start(f32[2,32,256]{2,1,0:T(8,128)S(1)} %broadcast_select_fusion.2), channel_id=1, source_target_pairs={{0,4},{4,8},{8,12},{12,16},{16,20},{20,24},{24,28},{1,5},{5,9},{9,... | collective-permute-start | bytes 196616 | tf_op jit(solution)/shard_map/while/body/eval_jaxpr/ppermute | solution.py:13
  69.8 13.4 %all_gather.15 = f32[4,2,32,128]{3,2,1,0:T(8,128)S(1)} all-gather(f32[1,2,32,128]{3,2,1,0:T(8,128)S(1)} %maximum_select_fusion.2), channel_id=1, replica_groups=mesh['row'=8,'col'=4] {'col'}, dimensions={0}, use_global_device_ids=true | all-gather | bytes 163840 | tf_op jit(solution)/shard_map/while/body/eval_jaxpr/all_gather | solution.py:18
  84.4 1.1 fusion.81
  85.5 1.1 fusion.84
  86.6 1.1 fusion.82
  87.7 4.9 %collective-permute-start = (f32[2,32,256]{2,1,0:T(8,128)S(1)}, f32[2,32,256]{2,1,0:T(8,128)S(1)}, u32[]{:S(2)}, u32[]{:S(2)}) collective-permute-start(f32[2,32,256]{2,1,0:T(8,128)S(1)} %broadcast_select_fusion.2), channel_id=1, source_target_pairs={{0,4},{4,8},{8,12},{12,16},{16,20},{20,24},{24,28},{1,5},{5,9},{9,... | collective-permute-start | bytes 196616 | tf_op jit(solution)/shard_map/while/body/eval_jaxpr/ppermute | solution.py:13
  98.5 13.4 %all_gather.15 = f32[4,2,32,128]{3,2,1,0:T(8,128)S(1)} all-gather(f32[1,2,32,128]{3,2,1,0:T(8,128)S(1)} %maximum_select_fusion.2), channel_id=1, replica_groups=mesh['row'=8,'col'=4] {'col'}, dimensions={0}, use_global_device_ids=true | all-gather | bytes 163840 | tf_op jit(solution)/shard_map/while/body/eval_jaxpr/all_gather | solution.py:18
  113.0 1.1 fusion.81
  114.1 1.1 fusion.84
  115.2 1.1 fusion.82
  116.4 5.0 %collective-permute-start = (f32[2,32,256]{2,1,0:T(8,128)S(1)}, f32[2,32,256]{2,1,0:T(8,128)S(1)}, u32[]{:S(2)}, u32[]{:S(2)}) collective-permute-start(f32[2,32,256]{2,1,0:T(8,128)S(1)} %broadcast_select_fusion.2), channel_id=1, source_target_pairs={{0,4},{4,8},{8,12},{12,16},{16,20},{20,24},{24,28},{1,5},{5,9},{9,... | collective-permute-start | bytes 196616 | tf_op jit(solution)/shard_map/while/body/eval_jaxpr/ppermute | solution.py:13
  127.2 13.4 %all_gather.15 = f32[4,2,32,128]{3,2,1,0:T(8,128)S(1)} all-gather(f32[1,2,32,128]{3,2,1,0:T(8,128)S(1)} %maximum_select_fusion.2), channel_id=1, replica_groups=mesh['row'=8,'col'=4] {'col'}, dimensions={0}, use_global_device_ids=true | all-gather | bytes 163840 | tf_op jit(solution)/shard_map/while/body/eval_jaxpr/all_gather | solution.py:18
  141.7 1.1 fusion.81
  142.8 1.1 fusion.84
  143.9 1.1 fusion.82
  145.1 4.2 %collective-permute-start = (f32[2,32,256]{2,1,0:T(8,128)S(1)}, f32[2,32,256]{2,1,0:T(8,128)S(1)}, u32[]{:S(2)}, u32[]{:S(2)}) collective-permute-start(f32[2,32,256]{2,1,0:T(8,128)S(1)} %broadcast_select_fusion.2), channel_id=1, source_target_pairs={{0,4},{4,8},{8,12},{12,16},{16,20},{20,24},{24,28},{1,5},{5,9},{9,... | collective-permute-start | bytes 196616 | tf_op jit(solution)/shard_map/while/body/eval_jaxpr/ppermute | solution.py:13
  155.1 13.4 %all_gather.15 = f32[4,2,32,128]{3,2,1,0:T(8,128)S(1)} all-gather(f32[1,2,32,128]{3,2,1,0:T(8,128)S(1)} %maximum_select_fusion.2), channel_id=1, replica_groups=mesh['row'=8,'col'=4] {'col'}, dimensions={0}, use_global_device_ids=true | all-gather | bytes 163840 | tf_op jit(solution)/shard_map/while/body/eval_jaxpr/all_gather | solution.py:18
  170.8 1.1 fusion.84
  171.9 1.1 fusion.82
  173.0 5.3 %collective-permute-start = (f32[2,32,256]{2,1,0:T(8,128)S(1)}, f32[2,32,256]{2,1,0:T(8,128)S(1)}, u32[]{:S(2)}, u32[]{:S(2)}) collective-permute-start(f32[2,32,256]{2,1,0:T(8,128)S(1)} %broadcast_select_fusion.2), channel_id=1, source_target_pairs={{0,4},{4,8},{8,12},{12,16},{16,20},{20,24},{24,28},{1,5},{5,9},{9,... | collective-permute-start | bytes 196616 | tf_op jit(solution)/shard_map/while/body/eval_jaxpr/ppermute | solution.py:13
  184.1 13.4 %all_gather.15 = f32[4,2,32,128]{3,2,1,0:T(8,128)S(1)} all-gather(f32[1,2,32,128]{3,2,1,0:T(8,128)S(1)} %maximum_select_fusion.2), channel_id=1, replica_groups=mesh['row'=8,'col'=4] {'col'}, dimensions={0}, use_global_device_ids=true | all-gather | bytes 163840 | tf_op jit(solution)/shard_map/while/body/eval_jaxpr/all_gather | solution.py:18
  199.8 1.1 fusion.84
  200.9 1.1 fusion.82
  202.0 5.1 %collective-permute-start = (f32[2,32,256]{2,1,0:T(8,128)S(1)}, f32[2,32,256]{2,1,0:T(8,128)S(1)}, u32[]{:S(2)}, u32[]{:S(2)}) collective-permute-start(f32[2,32,256]{2,1,0:T(8,128)S(1)} %broadcast_select_fusion.2), channel_id=1, source_target_pairs={{0,4},{4,8},{8,12},{12,16},{16,20},{20,24},{24,28},{1,5},{5,9},{9,... | collective-permute-start | bytes 196616 | tf_op jit(solution)/shard_map/while/body/eval_jaxpr/ppermute | solution.py:13
  213.0 13.4 %all_gather.15 = f32[4,2,32,128]{3,2,1,0:T(8,128)S(1)} all-gather(f32[1,2,32,128]{3,2,1,0:T(8,128)S(1)} %maximum_select_fusion.2), channel_id=1, replica_groups=mesh['row'=8,'col'=4] {'col'}, dimensions={0}, use_global_device_ids=true | all-gather | bytes 163840 | tf_op jit(solution)/shard_map/while/body/eval_jaxpr/all_gather | solution.py:18
  227.5 1.1 fusion.81
  228.6 1.1 fusion.84
  229.7 1.1 fusion.82
  230.9 6.9 %fusion.29 = f32[32,16384]{1,0:T(8,128)S(1)} fusion(f32[2,128,16384]{2,1,0:T(8,128)} %param.12, f32[2,32,128]{2,1,0:T(8,128)S(1)} %get-tuple-element.224), kind=kOutput, calls=%fused_computation.44 | convolution fusion | flops 805306368 | bytes 10502144 | tf_op jit(solution)/shard_map/dot_general | solution.py:22
  237.8 7.2 %fusion.31 = f32[32,16384]{1,0:T(8,128)S(1)} fusion(f32[2,128,16384]{2,1,0:T(8,128)} %param.12, f32[2,32,128]{2,1,0:T(8,128)S(1)} %get-tuple-element.224), kind=kOutput, calls=%fused_computation.46 | convolution fusion | flops 805306368 | bytes 10502144 | tf_op jit(solution)/shard_map/dot_general | solution.py:22
  245.0 4.4 %fusion.25 = f32[1,32,16384]{2,1,0:T(8,128)S(1)} fusion(f32[32,16384]{1,0:T(8,128)S(1)} %fusion.29, f32[2,128,16384]{2,1,0:T(8,128)S(1)} %copy-done.1, f32[2,32,128]{2,1,0:T(8,128)S(1)} %get-tuple-element.224), kind=kOutput, calls=%fused_computation.39 | convolution fusion | flops 805830656 | bytes 12599296 | tf_op jit(solution)/shard_map/dot_general | solution.py:22
  249.4 4.4 %fusion.26 = f32[1,32,16384]{2,1,0:T(8,128)S(1)} fusion(f32[32,16384]{1,0:T(8,128)S(1)} %fusion.31, f32[2,128,16384]{2,1,0:T(8,128)S(1)} %copy-done.1, f32[2,32,128]{2,1,0:T(8,128)S(1)} %get-tuple-element.224), kind=kOutput, calls=%fused_computation.41 | convolution fusion | flops 805830656 | bytes 12599296 | tf_op jit(solution)/shard_map/dot_general | solution.py:22
  253.9 2.2 pad_maximum_fusion
  257.2 51.2 %all-reduce = f32[128]{0:T(128)S(1)} all-reduce(f32[128]{0:T(128)S(1)} %convolution_bitcast_fusion), channel_id=3, replica_groups=mesh['row'=8,'col'=4] {'row','col'}, use_global_device_ids=true, to_apply=%region_5.6.clone | all-reduce | flops 128 | bytes 1024
  309.0 10.9 %reduce-scatter.2.cloned.1.call-done = f32[2,32,2048]{2,1,0:T(8,128)} async-done(((f32[2,32,16384]{2,1,0:T(8,128)}), f32[2,32,2048]{2,1,0:T(8,128)}) %reduce-scatter.2.cloned.1.call-update) | async-done | bytes 524304 | tf_op jit(solution)/shard_map/reduce_scatter | solution.py:58
  319.9 1.9 sub.46
  (116 shorter events, 57.7 us)
Async XLA Ops:
  7.2 249.7 %copy-start = (f32[2,128]{1,0:T(2,128)S(1)}, f32[2,128]{1,0:T(2,128)}, u32[]{:S(2)}) copy-start(f32[2,128]{1,0:T(2,128)} %param.14) | copy-start | bytes 3076
  7.2 312.7 %reduce-scatter.2.cloned.1.call-start = ((), (), s32[]{:S(2)}) async-start(), calls=%async_computation.1 | async-start | bytes 4718592 | tf_op jit(solution)/shard_map/reduce_scatter | solution.py:58
  7.3 3.3 %collective-permute-start = (f32[2,32,256]{2,1,0:T(8,128)S(1)}, f32[2,32,256]{2,1,0:T(8,128)S(1)}, u32[]{:S(2)}, u32[]{:S(2)}) collective-permute-start(f32[2,32,256]{2,1,0:T(8,128)S(1)} %broadcast_select_fusion.2), channel_id=1, source_target_pairs={{0,4},{4,8},{8,12},{12,16},{16,20},{20,24},{24,28},{1,5},{5,9},{9,... | collective-permute-start | bytes 196616 | tf_op jit(solution)/shard_map/while/body/eval_jaxpr/ppermute | solution.py:13
  34.4 2.3 collective-permute-start
  59.5 5.4 %collective-permute-start = (f32[2,32,256]{2,1,0:T(8,128)S(1)}, f32[2,32,256]{2,1,0:T(8,128)S(1)}, u32[]{:S(2)}, u32[]{:S(2)}) collective-permute-start(f32[2,32,256]{2,1,0:T(8,128)S(1)} %broadcast_select_fusion.2), channel_id=1, source_target_pairs={{0,4},{4,8},{8,12},{12,16},{16,20},{20,24},{24,28},{1,5},{5,9},{9,... | collective-permute-start | bytes 196616 | tf_op jit(solution)/shard_map/while/body/eval_jaxpr/ppermute | solution.py:13
  87.7 5.8 %collective-permute-start = (f32[2,32,256]{2,1,0:T(8,128)S(1)}, f32[2,32,256]{2,1,0:T(8,128)S(1)}, u32[]{:S(2)}, u32[]{:S(2)}) collective-permute-start(f32[2,32,256]{2,1,0:T(8,128)S(1)} %broadcast_select_fusion.2), channel_id=1, source_target_pairs={{0,4},{4,8},{8,12},{12,16},{16,20},{20,24},{24,28},{1,5},{5,9},{9,... | collective-permute-start | bytes 196616 | tf_op jit(solution)/shard_map/while/body/eval_jaxpr/ppermute | solution.py:13
  116.4 5.9 %collective-permute-start = (f32[2,32,256]{2,1,0:T(8,128)S(1)}, f32[2,32,256]{2,1,0:T(8,128)S(1)}, u32[]{:S(2)}, u32[]{:S(2)}) collective-permute-start(f32[2,32,256]{2,1,0:T(8,128)S(1)} %broadcast_select_fusion.2), channel_id=1, source_target_pairs={{0,4},{4,8},{8,12},{12,16},{16,20},{20,24},{24,28},{1,5},{5,9},{9,... | collective-permute-start | bytes 196616 | tf_op jit(solution)/shard_map/while/body/eval_jaxpr/ppermute | solution.py:13
  145.1 5.1 %collective-permute-start = (f32[2,32,256]{2,1,0:T(8,128)S(1)}, f32[2,32,256]{2,1,0:T(8,128)S(1)}, u32[]{:S(2)}, u32[]{:S(2)}) collective-permute-start(f32[2,32,256]{2,1,0:T(8,128)S(1)} %broadcast_select_fusion.2), channel_id=1, source_target_pairs={{0,4},{4,8},{8,12},{12,16},{16,20},{20,24},{24,28},{1,5},{5,9},{9,... | collective-permute-start | bytes 196616 | tf_op jit(solution)/shard_map/while/body/eval_jaxpr/ppermute | solution.py:13
  173.0 6.2 %collective-permute-start = (f32[2,32,256]{2,1,0:T(8,128)S(1)}, f32[2,32,256]{2,1,0:T(8,128)S(1)}, u32[]{:S(2)}, u32[]{:S(2)}) collective-permute-start(f32[2,32,256]{2,1,0:T(8,128)S(1)} %broadcast_select_fusion.2), channel_id=1, source_target_pairs={{0,4},{4,8},{8,12},{12,16},{16,20},{20,24},{24,28},{1,5},{5,9},{9,... | collective-permute-start | bytes 196616 | tf_op jit(solution)/shard_map/while/body/eval_jaxpr/ppermute | solution.py:13
  202.0 6.0 %collective-permute-start = (f32[2,32,256]{2,1,0:T(8,128)S(1)}, f32[2,32,256]{2,1,0:T(8,128)S(1)}, u32[]{:S(2)}, u32[]{:S(2)}) collective-permute-start(f32[2,32,256]{2,1,0:T(8,128)S(1)} %broadcast_select_fusion.2), channel_id=1, source_target_pairs={{0,4},{4,8},{8,12},{12,16},{16,20},{20,24},{24,28},{1,5},{5,9},{9,... | collective-permute-start | bytes 196616 | tf_op jit(solution)/shard_map/while/body/eval_jaxpr/ppermute | solution.py:13
  230.8 26.0 %copy-start.2 = (f32[2,32,128]{2,1,0:T(8,128)}, f32[2,32,128]{2,1,0:T(8,128)S(1)}, u32[]{:S(2)}) copy-start(f32[2,32,128]{2,1,0:T(8,128)S(1)} %get-tuple-element.224) | copy-start | bytes 98308
  230.9 14.2 %copy-start.1 = (f32[2,128,16384]{2,1,0:T(8,128)S(1)}, f32[2,128,16384]{2,1,0:T(8,128)}, u32[]{:S(2)}) copy-start(f32[2,128,16384]{2,1,0:T(8,128)} %param.12) | copy-start | bytes 50331652
  256.1 0.7 copy-start.4
  256.1 63.8 %copy-start.3 = (f32[2,32,2048]{2,1,0:T(8,128)S(1)}, f32[2,32,2048]{2,1,0:T(8,128)}, u32[]{:S(2)}) copy-start(f32[2,32,2048]{2,1,0:T(8,128)} %param.13) | copy-start | bytes 1572868
Sparse Core Ops, SparseCore 0:
  256.2 63.6 reduce-scatter.1
